TPU v7x, 32 devices: a whole 2x2x4 slice. The times are simulated.
32 devices in a mesh: seq: 8 (over y, x, core), tp: 4 (over z).
Axes of the slice: x: 2, y: 2, z: 4, core: 2. Of those that a mesh axis runs over, the one named last changes fastest.
Arguments:
- tokens: bfloat16 [128, 17, 1152], P('seq'), may hold values from -6 to 6
- cotangent: bfloat16 [128, 17, 1152], P('seq'), may hold values from -6 to 6
- caption: bfloat16 [4, 300, 1152], replicated, may hold values from -6 to 6
- condition: float32 [4, 1152], replicated, may hold values from -6 to 6
- frames: int32 [4], replicated, may hold values from 1 to 17, 44 in all
- cap_len: int32 [4], replicated, may hold values from 1 to 300, 600 in all
- clip_of: int32 [128], P('seq'), may hold values from 0 to 3
- w_qkv: bfloat16 [1152, 3, 1152], P('seq', None, 'tp'), may hold values from -0.1875 to 0.1875
- w_out: bfloat16 [1152, 1152], P('tp', 'seq'), may hold values from -0.375 to 0.375
- w_query2: bfloat16 [1152, 1152], P('seq', 'tp'), may hold values from -0.1875 to 0.1875
- w_kv2: bfloat16 [1152, 2, 1152], P('seq', None, 'tp'), may hold values from -0.1875 to 0.1875
- w_out2: bfloat16 [1152, 1152], P('tp', 'seq'), may hold values from -0.75 to 0.75
- w_up: bfloat16 [1152, 4608], P('seq', 'tp'), may hold values from -0.1875 to 0.1875
- w_down: bfloat16 [4608, 1152], P('tp', 'seq'), may hold values from -0.09375 to 0.09375
- w_ada: bfloat16 [1152, 6912], P('seq', 'tp'), may hold values from -0.1875 to 0.1875
Outputs:
- output: bfloat16 [128, 17, 1152], P('seq')
- d_tokens: bfloat16 [128, 17, 1152], P('seq')
- d_caption: float32 [4, 300, 1152], P(None, None, 'tp')
- d_condition: float32 [4, 1152], replicated
- d_w_qkv: float32 [1152, 3, 1152], P('seq', None, 'tp')
- d_w_out: float32 [1152, 1152], P('tp', 'seq')
- d_w_query2: float32 [1152, 1152], P('seq', 'tp')
- d_w_kv2: float32 [1152, 2, 1152], P('seq', None, 'tp')
- d_w_out2: float32 [1152, 1152], P('tp', 'seq')
- d_w_up: float32 [1152, 4608], P('seq', 'tp')
- d_w_down: float32 [4608, 1152], P('tp', 'seq')
- d_w_ada: float32 [1152, 6912], P('seq', 'tp')
Inputs may be any that keep to these rules, and one draw needn't show every extreme that they name: frames of each clip; they add up to 44 and one clip has 17. `cap_len`: live caption tokens of each clip, the first ones of its slots; they add up to 600 and one clip has 300.
All inputs are finite; a program needn't handle non-finite values.
Results may differ from a plain program's by a relative error of at most 0.024.
Values may be sent and summed in bfloat16 or wider, within the bound.
No kernel may reach another device: no remote copies, remote signals or barrier semaphores. Data moves between devices by JAX's collectives and lax.ppermute only.
A program may use at most 128 MiB of HBM per device.

v0:
```python
import jax
import jax.numpy as jnp
from jax import lax
from jax.sharding import PartitionSpec as P

HDIM = 72
CLIPS = 4
EPSILON = 1e-06
NEG_FILL = -1e30
HIGHEST = lax.Precision.HIGHEST


def normalize(rows):
    center = rows - jnp.mean(rows, -1, keepdims=True)
    return center * lax.rsqrt(jnp.mean(center * center, -1, keepdims=True) + EPSILON)


def modulate(rows, shift, scale):
    return normalize(rows) * (1.0 + scale[:, None, :]) + shift[:, None, :]


def total_rows(partial_value):
    return lax.psum(partial_value, "tp")


def frame_attention(triple, live, head_scale):
    raw = (
        jnp.einsum(
            "lfhe,lghe->lhfg", triple[:, :, 0], triple[:, :, 1], preferred_element_type=jnp.float32
        )
        * head_scale
    )
    probs = jax.nn.softmax(jnp.where(live[:, None, None, :], raw, NEG_FILL), axis=-1)
    result = jnp.einsum(
        "lhfg,lghe->lfhe",
        probs.astype(jnp.bfloat16),
        triple[:, :, 2],
        preferred_element_type=jnp.float32,
    )
    return (probs, result.astype(jnp.bfloat16))


def cross_scores(query, keys, clips, key_clip, key_live, head_scale):
    raw = jnp.einsum("rhe,khe->hrk", query, keys, preferred_element_type=jnp.float32) * head_scale
    allowed = (clips[:, None] == key_clip[None, :]) & key_live[None, :]
    return jnp.where(allowed[None], raw, NEG_FILL)


def shards(
    tokens,
    cotangent,
    caption,
    condition,
    frames,
    cap_len,
    clip_of,
    w_qkv,
    w_out,
    w_query2,
    w_kv2,
    w_out2,
    w_up,
    w_down,
    w_ada,
):
    seqs, fmax, width = tokens.shape
    row_count = seqs * fmax
    inner = w_qkv.shape[2]
    local_heads = inner // HDIM
    head_scale = HDIM ** (-0.5)
    full_qkv, full_out, full_query2, full_kv2, full_out2, full_up, full_down, full_ada = (
        lax.all_gather(w_qkv, "seq", axis=0, tiled=True),
        lax.all_gather(w_out, "seq", axis=1, tiled=True),
        lax.all_gather(w_query2, "seq", axis=0, tiled=True),
        lax.all_gather(w_kv2, "seq", axis=0, tiled=True),
        lax.all_gather(w_out2, "seq", axis=1, tiled=True),
        lax.all_gather(w_up, "seq", axis=0, tiled=True),
        lax.all_gather(w_down, "seq", axis=1, tiled=True),
        lax.all_gather(w_ada, "seq", axis=0, tiled=True),
    )
    qkv_matrix = full_qkv.reshape(width, 3 * inner)
    kv_matrix = full_kv2.reshape(width, 2 * inner)
    scaled = jax.nn.silu(condition).astype(jnp.bfloat16)
    mod_part = jnp.dot(scaled, full_ada, preferred_element_type=jnp.float32)
    mods = lax.all_gather(mod_part, "tp", axis=1, tiled=True).reshape(CLIPS, 6, width)
    clip_ids = jnp.arange(CLIPS)
    clip_hot = clip_of[:, None] == clip_ids[None, :]
    seq_mods = jnp.sum(jnp.where(clip_hot[:, :, None, None], mods[None], 0.0), 1)
    seq_frames = jnp.sum(jnp.where(clip_hot, frames[None, :], 0), 1)
    live = jnp.arange(fmax)[None, :] < seq_frames[:, None]
    own_live = live.astype(jnp.float32)[:, :, None]
    own_hot = clip_hot.astype(jnp.float32)
    key_count = caption.shape[0] * caption.shape[1]
    key_clip = jnp.arange(key_count) // caption.shape[1]
    key_len = jnp.sum(jnp.where(key_clip[:, None] == clip_ids[None, :], cap_len[None, :], 0), 1)
    key_live = jnp.arange(key_count) % caption.shape[1] < key_len
    row_clip = jnp.repeat(clip_of, fmax)
    block_seqs = min(32, seqs)
    blocks = seqs // block_seqs
    block_rows = block_seqs * fmax
    block_clip = row_clip.reshape(blocks, block_rows)
    own_input = tokens.astype(jnp.float32)
    attn_in = (
        modulate(own_input, seq_mods[:, 0], seq_mods[:, 1])
        .astype(jnp.bfloat16)
        .reshape(row_count, width)
    )
    triple = (
        jnp.dot(attn_in, qkv_matrix, preferred_element_type=jnp.float32)
        .astype(jnp.bfloat16)
        .reshape(seqs, fmax, 3, local_heads, HDIM)
    )
    probs, frame_out = frame_attention(triple, live, head_scale)
    frame_out = frame_out.reshape(row_count, inner)
    branch_one = total_rows(
        jnp.dot(frame_out, full_out, preferred_element_type=jnp.float32).reshape(seqs, fmax, width)
    )
    first = own_input + seq_mods[:, 2][:, None, :] * branch_one
    first_low = first.astype(jnp.bfloat16).reshape(row_count, width)
    cross_query = (
        jnp.dot(first_low, full_query2, preferred_element_type=jnp.float32)
        .astype(jnp.bfloat16)
        .reshape(blocks, block_rows, local_heads, HDIM)
    )
    cross_kv = (
        jnp.dot(caption.reshape(key_count, width), kv_matrix, preferred_element_type=jnp.float32)
        .astype(jnp.bfloat16)
        .reshape(key_count, 2, local_heads, HDIM)
    )
    cross_key = cross_kv[:, 0]
    cross_value = cross_kv[:, 1]

    def cross_block(pair):
        query, clips = pair
        scores = cross_scores(query, cross_key, clips, key_clip, key_live, head_scale)
        top = jnp.max(scores, -1, keepdims=True)
        weights = jnp.exp(scores - top)
        denom = jnp.sum(weights, -1, keepdims=True)
        block_out = jnp.einsum(
            "hrk,khe->rhe",
            (weights / denom).astype(jnp.bfloat16),
            cross_value,
            preferred_element_type=jnp.float32,
        )
        return (block_out.astype(jnp.bfloat16), (top + jnp.log(denom))[..., 0])

    cross_out, cross_lse = lax.map(cross_block, (cross_query, block_clip))
    cross_out = cross_out.reshape(row_count, inner)
    second = first + total_rows(
        jnp.dot(cross_out, full_out2, preferred_element_type=jnp.float32).reshape(seqs, fmax, width)
    )
    mlp_in = (
        modulate(second, seq_mods[:, 3], seq_mods[:, 4])
        .astype(jnp.bfloat16)
        .reshape(row_count, width)
    )
    hidden_pre = jnp.dot(mlp_in, full_up, preferred_element_type=jnp.float32)
    hidden = jax.nn.gelu(hidden_pre, approximate=True).astype(jnp.bfloat16)
    branch_three = total_rows(
        jnp.dot(hidden, full_down, preferred_element_type=jnp.float32).reshape(seqs, fmax, width)
    )
    third = second + seq_mods[:, 5][:, None, :] * branch_three
    output = (third * own_live).astype(jnp.bfloat16)
    grad_three = cotangent.astype(jnp.float32) * own_live
    d_branch3 = (
        (seq_mods[:, 5][:, None, :] * grad_three).astype(jnp.bfloat16).reshape(row_count, width)
    )
    grad_down = jnp.einsum("rk,rd->kd", hidden, d_branch3, preferred_element_type=jnp.float32)
    d_hidden = jnp.einsum("rd,kd->rk", d_branch3, full_down, preferred_element_type=jnp.float32)
    gelu_pull = jax.vjp(lambda value: jax.nn.gelu(value, approximate=True), hidden_pre)[1]
    d_pre = gelu_pull(d_hidden)[0].astype(jnp.bfloat16)
    grad_up = jnp.einsum("rd,rk->dk", mlp_in, d_pre, preferred_element_type=jnp.float32)
    d_mlp = total_rows(
        jnp.einsum("rk,dk->rd", d_pre, full_up, preferred_element_type=jnp.float32).reshape(
            seqs, fmax, width
        )
    )
    second_pull = jax.vjp(modulate, second, seq_mods[:, 3], seq_mods[:, 4])[1]
    norm_two, d_shift2, d_scale2 = second_pull(d_mlp)
    grad_two = grad_three + norm_two
    d_branch2 = grad_two.astype(jnp.bfloat16).reshape(row_count, width)
    grad_out2 = jnp.einsum("rc,rd->cd", cross_out, d_branch2, preferred_element_type=jnp.float32)
    d_cross = (
        jnp.einsum("rd,cd->rc", d_branch2, full_out2, preferred_element_type=jnp.float32)
        .astype(jnp.bfloat16)
        .reshape(blocks, block_rows, local_heads, HDIM)
    )

    def cross_back(carry, item):
        key_sum, value_sum = carry
        query, clips, block_lse, grad_block = item
        scores = cross_scores(query, cross_key, clips, key_clip, key_live, head_scale)
        weights = jnp.exp(scores - block_lse[..., None])
        value_sum = value_sum + jnp.einsum(
            "hrk,rhe->khe",
            weights.astype(jnp.bfloat16),
            grad_block,
            preferred_element_type=jnp.float32,
        )
        grad_weights = jnp.einsum(
            "rhe,khe->hrk", grad_block, cross_value, preferred_element_type=jnp.float32
        )
        grad_scores = (
            weights * (grad_weights - jnp.sum(weights * grad_weights, -1, keepdims=True))
        ).astype(jnp.bfloat16)
        grad_query = (
            jnp.einsum("hrk,khe->rhe", grad_scores, cross_key, preferred_element_type=jnp.float32)
            * head_scale
        ).astype(jnp.bfloat16)
        key_sum = (
            key_sum
            + jnp.einsum("hrk,rhe->khe", grad_scores, query, preferred_element_type=jnp.float32)
            * head_scale
        )
        return ((key_sum, value_sum), grad_query)

    zero_keys = jnp.zeros((key_count, local_heads, HDIM), jnp.float32)
    (key_grad, value_grad), d_query = lax.scan(
        cross_back, (zero_keys, zero_keys), (cross_query, block_clip, cross_lse, d_cross)
    )
    d_query = d_query.reshape(row_count, inner)
    grad_query2 = jnp.einsum("rd,rc->dc", first_low, d_query, preferred_element_type=jnp.float32)
    grad_one = grad_two + total_rows(
        jnp.einsum("rc,dc->rd", d_query, full_query2, preferred_element_type=jnp.float32).reshape(
            seqs, fmax, width
        )
    )
    d_branch1 = (
        (seq_mods[:, 2][:, None, :] * grad_one).astype(jnp.bfloat16).reshape(row_count, width)
    )
    grad_out = jnp.einsum("rc,rd->cd", frame_out, d_branch1, preferred_element_type=jnp.float32)
    d_frame = (
        jnp.einsum("rd,cd->rc", d_branch1, full_out, preferred_element_type=jnp.float32)
        .astype(jnp.bfloat16)
        .reshape(seqs, fmax, local_heads, HDIM)
    )
    d_value = jnp.einsum(
        "lhfg,lfhe->lghe", probs.astype(jnp.bfloat16), d_frame, preferred_element_type=jnp.float32
    )
    d_probs = jnp.einsum(
        "lfhe,lghe->lhfg", d_frame, triple[:, :, 2], preferred_element_type=jnp.float32
    )
    d_scores = (probs * (d_probs - jnp.sum(probs * d_probs, -1, keepdims=True))).astype(
        jnp.bfloat16
    )
    d_queries = (
        jnp.einsum("lhfg,lghe->lfhe", d_scores, triple[:, :, 1], preferred_element_type=jnp.float32)
        * head_scale
    )
    d_keys = (
        jnp.einsum("lhfg,lfhe->lghe", d_scores, triple[:, :, 0], preferred_element_type=jnp.float32)
        * head_scale
    )
    d_triple = (
        jnp.stack([d_queries, d_keys, d_value], 2)
        .astype(jnp.bfloat16)
        .reshape(row_count, 3 * inner)
    )
    grad_qkv = jnp.einsum(
        "rd,rc->dc", attn_in, d_triple, preferred_element_type=jnp.float32
    ).reshape(width, 3, inner)
    d_attn = total_rows(
        jnp.einsum("rc,dc->rd", d_triple, qkv_matrix, preferred_element_type=jnp.float32).reshape(
            seqs, fmax, width
        )
    )
    first_pull = jax.vjp(modulate, own_input, seq_mods[:, 0], seq_mods[:, 1])[1]
    norm_one, d_shift1, d_scale1 = first_pull(d_attn)
    d_tokens = (grad_one + norm_one).astype(jnp.bfloat16)
    d_gate1 = jnp.sum(grad_one * branch_one, 1)
    d_gate2 = jnp.sum(grad_three * branch_three, 1)
    seq_terms = jnp.stack([d_shift1, d_scale1, d_gate1, d_shift2, d_scale2, d_gate2], 1)
    d_mods = jnp.einsum("lc,ljd->cjd", own_hot, seq_terms, precision=HIGHEST).reshape(
        CLIPS, 6 * width
    )
    kv_grad = jnp.stack([key_grad, value_grad], 1)
    kv_total, mods_total = (
        lax.psum(kv_grad.astype(jnp.bfloat16), "seq").astype(jnp.float32),
        lax.psum(d_mods.astype(jnp.bfloat16), "seq").astype(jnp.float32),
    )
    col_count = mods_total.shape[1] // lax.axis_size("tp")
    mod_cols = lax.dynamic_slice_in_dim(mods_total, lax.axis_index("tp") * col_count, col_count, 1)
    seq_rows = w_ada.shape[0]
    seq_start = lax.axis_index("seq") * seq_rows
    scaled_rows = lax.dynamic_slice_in_dim(scaled, seq_start, seq_rows, 1).astype(jnp.float32)
    grad_ada = jnp.einsum("cd,ck->dk", scaled_rows, mod_cols, precision=HIGHEST)
    silu_pull = jax.vjp(jax.nn.silu, condition)[1]
    cond_part = silu_pull(
        jnp.einsum("ck,dk->cd", mod_cols, full_ada.astype(jnp.float32), precision=HIGHEST)
    )[0]
    d_condition = lax.psum(cond_part, "tp")
    kv_low = kv_total.astype(jnp.bfloat16).reshape(key_count, 2 * inner)
    caption_rows = lax.dynamic_slice_in_dim(
        caption.reshape(key_count, width), seq_start, seq_rows, 1
    )
    grad_kv2 = jnp.einsum(
        "kd,kc->dc", caption_rows, kv_low, preferred_element_type=jnp.float32
    ).reshape(seq_rows, 2, inner)
    caption_part = jnp.einsum(
        "kc,dc->kd", kv_low, kv_matrix, preferred_element_type=jnp.float32
    ).reshape(caption.shape)
    d_caption = lax.psum_scatter(
        caption_part.astype(jnp.bfloat16), "tp", scatter_dimension=2, tiled=True
    ).astype(jnp.float32)
    summed = (
        lax.psum_scatter(
            grad_qkv.astype(jnp.bfloat16), "seq", scatter_dimension=0, tiled=True
        ).astype(jnp.float32),
        lax.psum_scatter(
            grad_out.astype(jnp.bfloat16), "seq", scatter_dimension=1, tiled=True
        ).astype(jnp.float32),
        lax.psum_scatter(
            grad_query2.astype(jnp.bfloat16), "seq", scatter_dimension=0, tiled=True
        ).astype(jnp.float32),
        lax.psum_scatter(
            grad_out2.astype(jnp.bfloat16), "seq", scatter_dimension=1, tiled=True
        ).astype(jnp.float32),
        lax.psum_scatter(
            grad_up.astype(jnp.bfloat16), "seq", scatter_dimension=0, tiled=True
        ).astype(jnp.float32),
        lax.psum_scatter(
            grad_down.astype(jnp.bfloat16), "seq", scatter_dimension=1, tiled=True
        ).astype(jnp.float32),
    )
    return (
        output,
        d_tokens,
        d_caption,
        d_condition,
        summed[0],
        summed[1],
        summed[2],
        grad_kv2,
        summed[3],
        summed[4],
        summed[5],
        grad_ada,
    )


def solution(mesh):
    return jax.shard_map(
        shards,
        mesh=mesh,
        in_specs=(
            P("seq", None, None),
            P("seq", None, None),
            P(),
            P(),
            P(),
            P(),
            P("seq"),
            P("seq", None, "tp"),
            P("tp", "seq"),
            P("seq", "tp"),
            P("seq", None, "tp"),
            P("tp", "seq"),
            P("seq", "tp"),
            P("tp", "seq"),
            P("seq", "tp"),
        ),
        out_specs=(
            P("seq", None, None),
            P("seq", None, None),
            P(None, None, "tp"),
            P(),
            P("seq", None, "tp"),
            P("tp", "seq"),
            P("seq", "tp"),
            P("seq", None, "tp"),
            P("tp", "seq"),
            P("seq", "tp"),
            P("tp", "seq"),
            P("seq", "tp"),
        ),
        check_vma=False,
    )
```

profile of v0, /device:TPU:0, one launch (start us, length us, event | category | flops | bytes accessed | tf_op | source)
XLA Modules:
  0.0 1068.3 jit_solution(13612882484881826433)
XLA Ops:
  14.8 15.0 %all_gather.30 = bf16[288,1152]{0,1:T(8,128)(2,1)S(1)} all-gather(bf16[288,144]{0,1:T(8,128)(2,1)S(1)} %copy-done.45), channel_id=1, replica_groups=mesh['seq'=8,'tp'=4] {'seq'}, dimensions={1}, use_global_device_ids=true | all-gather | bytes 746496 | tf_op jit(solution)/shard_map/all_gather | solution.py:73
  29.7 13.7 %all_gather.32 = bf16[1152,288]{1,0:T(8,128)(2,1)S(1)} all-gather(bf16[144,288]{1,0:T(8,128)(2,1)S(1)} %copy-done.46), channel_id=1, replica_groups=mesh['seq'=8,'tp'=4] {'seq'}, dimensions={0}, use_global_device_ids=true | all-gather | bytes 746496 | tf_op jit(solution)/shard_map/all_gather | solution.py:74
  43.4 11.3 %all_gather.33 = bf16[288,1152]{0,1:T(8,128)(2,1)} all-gather(bf16[288,144]{0,1:T(8,128)(2,1)S(1)} %copy-done.47), channel_id=1, replica_groups=mesh['seq'=8,'tp'=4] {'seq'}, dimensions={1}, use_global_device_ids=true | all-gather | bytes 746496 | tf_op jit(solution)/shard_map/all_gather | solution.py:76
  56.6 3.3 reshape.348
  59.9 4.3 copy.144
  64.2 21.8 %all-gather.7.cloned.1.call-done = bf16[1152,1728]{1,0:T(8,128)(2,1)} async-done(((bf16[144,1728]{1,0:T(8,128)(2,1)}), bf16[1152,1728]{1,0:T(8,128)(2,1)}) %all-gather.7.cloned.1.call-update) | async-done | bytes 3981328 | tf_op jit(solution)/shard_map/all_gather | solution.py:79
  86.0 2.8 convolution_bitcast_fusion
  88.8 13.4 %all-gather = f32[4,1728,4]{1,2,0:T(4,128)S(1)} all-gather(f32[1,1728,4]{1,2,0:T(4,128)S(1)} %convolution_bitcast_fusion), channel_id=1, replica_groups=mesh['seq'=8,'tp'=4] {'tp'}, dimensions={0}, use_global_device_ids=true | all-gather | bytes 138240 | tf_op jit(solution)/shard_map/all_gather | solution.py:85
  105.5 3.5 convolution_convert_fusion.9
  109.0 2.9 reshape.347
  115.8 2.7 fusion.37
  123.3 5.6 copy.152
  128.9 5.6 convolution_convert_fusion.4
  134.5 63.4 %all-reduce.8.cloned.1.call-done = f32[16,17,1152]{2,1,0:T(8,128)} async-done(((f32[16,17,1152]{2,1,0:T(8,128)}), f32[16,17,1152]{2,1,0:T(8,128)}) %all-reduce.8.cloned.1.call-update) | async-done | bytes 1253392 | tf_op jit(solution)/shard_map/psum | solution.py:23
  201.1 2.5 fusion.98
  212.2 73.3 %all-reduce.10.cloned.1.call-done = f32[16,17,1152]{2,1,0:T(8,128)} async-done(((f32[16,17,1152]{2,1,0:T(8,128)}), f32[16,17,1152]{2,1,0:T(8,128)}) %all-reduce.10.cloned.1.call-update) | async-done | bytes 1253392 | tf_op jit(solution)/shard_map/psum | solution.py:23
  285.5 2.5 fusion.94
  291.0 2.2 reshape.354
  293.2 2.3 reshape.352
  295.4 21.2 %all-gather.15.cloned.1.call-done = bf16[1152,1152]{0,1:T(8,128)(2,1)} async-done(((bf16[1152,144]{0,1:T(8,128)(2,1)}), bf16[1152,1152]{0,1:T(8,128)(2,1)}) %all-gather.15.cloned.1.call-update) | async-done | bytes 2654224 | tf_op jit(solution)/shard_map/all_gather | solution.py:78
  316.6 4.1 fusion.99
  320.7 28.1 %all-gather.13.cloned.1.call-done = bf16[1152,1152]{1,0:T(8,128)(2,1)} async-done(((bf16[144,1152]{1,0:T(8,128)(2,1)}), bf16[1152,1152]{1,0:T(8,128)(2,1)}) %all-gather.13.cloned.1.call-update) | async-done | bytes 2654224 | tf_op jit(solution)/shard_map/all_gather | solution.py:77
  348.8 5.0 fusion.36
  354.6 2.2 fusion.100
  356.8 2.7 reshape.355
  359.8 75.4 %all-reduce.12.cloned.1.call-done = f32[16,17,1152]{2,1,0:T(8,128)} async-done(((f32[16,17,1152]{2,1,0:T(8,128)}), f32[16,17,1152]{2,1,0:T(8,128)}) %all-reduce.12.cloned.1.call-update) | async-done | bytes 1253392 | tf_op jit(solution)/shard_map/psum | solution.py:23
  435.2 3.3 multiply_reduce_fusion.2
  441.6 2.2 reshape.356
  443.8 2.6 convolution_convert_fusion.12
  447.5 4.6 multiply_reduce_fusion
  458.0 3.1 fusion.44
  461.2 2.7 fusion.15
  463.9 4.0 fusion.16
  469.2 2.9 convolution_convert_fusion.5
  473.1 2.8 convolution_convert_fusion.6
  476.0 59.8 %all-reduce.14.cloned.1.call-done = f32[16,17,1152]{2,1,0:T(8,128)} async-done(((f32[16,17,1152]{2,1,0:T(8,128)}), f32[16,17,1152]{2,1,0:T(8,128)}) %all-reduce.14.cloned.1.call-update) | async-done | bytes 1253392 | tf_op jit(solution)/shard_map/psum | solution.py:23
  535.8 3.9 multiply_reduce_fusion.3
  542.0 2.2 reshape.357
  544.2 2.7 convolution_convert_fusion.7
  547.4 4.5 convolution_convert_fusion.1
  552.0 4.7 convolution_convert_fusion
  556.8 4.5 fusion.91
  561.3 2.7 reshape.353
  574.7 2.9 reshape.378
  577.6 4.3 fusion.101
  582.1 2.2 reshape.375
  587.4 4.5 convolution_convert_fusion.3
  591.9 4.7 all-reduce.16.cloned.1.call-done
  596.6 2.6 fusion.52
  600.2 4.2 dot_general.164
  604.5 6.6 convolution_convert_fusion.2
  611.1 23.5 %reduce-scatter.16.cloned.1.call-done = bf16[288,144]{0,1:T(8,128)(2,1)} async-done(((bf16[288,1152]{0,1:T(8,128)(2,1)}), bf16[288,144]{0,1:T(8,128)(2,1)}) %reduce-scatter.16.cloned.1.call-update) | async-done | bytes 82960 | tf_op jit(solution)/shard_map/reduce_scatter | solution.py:315
  636.2 36.7 %reduce-scatter.14.cloned.1.call-done = bf16[144,288]{1,0:T(8,128)(2,1)} async-done(((bf16[1152,288]{1,0:T(8,128)(2,1)}), bf16[144,288]{1,0:T(8,128)(2,1)}) %reduce-scatter.14.cloned.1.call-update) | async-done | bytes 82960 | tf_op jit(solution)/shard_map/reduce_scatter | solution.py:312
  674.4 37.7 %reduce-scatter.12.cloned.1.call-done = bf16[288,144]{0,1:T(8,128)(2,1)} async-done(((bf16[288,1152]{0,1:T(8,128)(2,1)}), bf16[288,144]{0,1:T(8,128)(2,1)}) %reduce-scatter.12.cloned.1.call-update) | async-done | bytes 82960 | tf_op jit(solution)/shard_map/reduce_scatter | solution.py:309
  713.7 45.6 %reduce-scatter.18.cloned.1.call-done = bf16[144,1152]{1,0:T(8,128)(2,1)} async-done(((bf16[1152,1152]{1,0:T(8,128)(2,1)}), bf16[144,1152]{1,0:T(8,128)(2,1)}) %reduce-scatter.18.cloned.1.call-update) | async-done | bytes 331792 | tf_op jit(solution)/shard_map/reduce_scatter | solution.py:318
  761.2 45.7 %reduce-scatter.20.cloned.1.call-done = bf16[1152,144]{0,1:T(8,128)(2,1)} async-done(((bf16[1152,1152]{0,1:T(8,128)(2,1)}), bf16[1152,144]{0,1:T(8,128)(2,1)}) %reduce-scatter.20.cloned.1.call-update) | async-done | bytes 331792 | tf_op jit(solution)/shard_map/reduce_scatter | solution.py:321
  808.7 135.2 %all-reduce.18.cloned.1.call-done = (f32[16,17,1152]{2,1,0:T(8,128)}, f32[16,17,1152]{2,1,0:T(8,128)}) async-done(((f32[16,17,1152]{2,1,0:T(8,128)}, f32[16,17,1152]{2,1,0:T(8,128)}), (f32[16,17,1152]{2,1,0:T(8,128)}, f32[16,17,1152]{2,1,0:T(8,128)})) %all-reduce.18.cloned.1.call-update) | async-done | bytes 2506768 | tf_op jit(solution)/shard_map/psum | solution.py:23
  943.9 2.1 fusion.25
  951.2 24.9 %psum.70 = bf16[4,6912]{1,0:T(4,128)(2,1)S(1)} all-reduce(bf16[4,6912]{1,0:T(4,128)(2,1)S(1)} %bitcast.198), channel_id=1, replica_groups=mesh['seq'=8,'tp'=4] {'seq'}, use_global_device_ids=true, to_apply=%region_31.32 | all-reduce | flops 27648 | bytes 110592 | tf_op jit(solution)/shard_map/psum | solution.py:279
  976.1 3.4 fusion.68
  979.5 17.6 %psum.71 = f32[4,1152]{1,0:T(4,128)} all-reduce(f32[4,1152]{1,0:T(4,128)S(1)} %fusion.68), channel_id=1, replica_groups=mesh['seq'=8,'tp'=4] {'tp'}, use_global_device_ids=true, to_apply=%region_32.33 | all-reduce | flops 4608 | bytes 36864 | tf_op jit(solution)/shard_map/psum | solution.py:291
  997.1 2.0 fusion.73
  1001.1 57.7 %reduce-scatter.8.cloned.1.call-done = bf16[4,300,288]{1,2,0:T(8,128)(2,1)} async-done(((bf16[4,300,1152]{1,2,0:T(8,128)(2,1)}), bf16[4,300,288]{1,2,0:T(8,128)(2,1)}) %reduce-scatter.8.cloned.1.call-update) | async-done | bytes 691216 | tf_op jit(solution)/shard_map/reduce_scatter | solution.py:302
  1058.8 2.5 convert_element_type.205
  (261 shorter events, 82.6 us)
Async XLA Ops:
  7.2 6.5 copy-start.1
  7.2 7.5 copy-start.48
  7.2 7.6 copy-start.45
  7.2 22.5 %copy-start.46 = (bf16[144,288]{1,0:T(8,128)(2,1)S(1)}, bf16[144,288]{1,0:T(8,128)(2,1)}, u32[]{:S(2)}) copy-start(bf16[144,288]{1,0:T(8,128)(2,1)} %param.24) | copy-start | bytes 248836
  7.2 52.7 %all-gather.9.cloned.1.call-start = ((), (), s32[]{:S(2)}) async-start(), calls=%async_computation.8 | async-start | bytes 2985984 | tf_op jit(solution)/shard_map/all_gather | solution.py:72
  8.0 78.0 %all-gather.7.cloned.1.call-start = ((), (), s32[]{:S(2)}) async-start(), calls=%async_computation.7 | async-start | bytes 4644864 | tf_op jit(solution)/shard_map/all_gather | solution.py:79
  8.7 34.7 %copy-start.47 = (bf16[288,144]{0,1:T(8,128)(2,1)S(1)}, bf16[288,144]{0,1:T(8,128)(2,1)}, u32[]{:S(2)}) copy-start(bf16[288,144]{0,1:T(8,128)(2,1)} %param.26) | copy-start | bytes 248836
  8.7 114.6 %all-gather.11.cloned.1.call-start = ((), (), s32[]{:S(2)}) async-start(), calls=%async_computation.10 | async-start | bytes 1990656 | tf_op jit(solution)/shard_map/all_gather | solution.py:75
  9.5 188.4 %all-reduce.8.cloned.1.call-start = ((), (), s32[]{:S(2)}) async-start(), calls=%async_computation.9 | async-start | bytes 3538944 | tf_op jit(solution)/shard_map/psum | solution.py:23
  13.6 41.1 %copy-start.17 = (bf16[4,300,1152]{2,0,1:T(4,128)(2,1)S(1)}, bf16[4,300,1152]{2,0,1:T(4,128)(2,1)}, u32[]{:S(2)}) copy-start(bf16[4,300,1152]{2,0,1:T(4,128)(2,1)} %param.17) | copy-start | bytes 8294404
  14.7 71.3 %copy-start.56 = (bf16[4,1152]{1,0:T(4,128)(2,1)}, bf16[4,1152]{1,0:T(4,128)(2,1)S(1)}, u32[]{:S(2)}) copy-start(bf16[4,1152]{1,0:T(4,128)(2,1)S(1)} %multiply_convert_fusion.6) | copy-start | bytes 27652
  29.7 90.2 %copy-start.9 = (bf16[288,1152]{0,1:T(8,128)(2,1)}, bf16[288,1152]{0,1:T(8,128)(2,1)S(1)}, u32[]{:S(2)}) copy-start(bf16[288,1152]{0,1:T(8,128)(2,1)S(1)} %all_gather.30) | copy-start | bytes 1990660
  43.4 156.5 %copy-start.10 = (bf16[1152,288]{1,0:T(8,128)(2,1)}, bf16[1152,288]{1,0:T(8,128)(2,1)S(1)}, u32[]{:S(2)}) copy-start(bf16[1152,288]{1,0:T(8,128)(2,1)S(1)} %all_gather.32) | copy-start | bytes 1990660
  103.3 182.3 %copy-start.31 = (f32[16,1152]{1,0:T(8,128)}, f32[16,1152]{1,0:T(8,128)S(1)}, u32[]{:S(2)}) copy-start(f32[16,1152]{1,0:T(8,128)S(1)} %get-tuple-element.159) | copy-start | bytes 221188
  103.3 185.1 %copy-start.36 = (f32[16,1152]{1,0:T(8,128)}, f32[16,1152]{1,0:T(8,128)S(1)}, u32[]{:S(2)}) copy-start(f32[16,1152]{1,0:T(8,128)S(1)} %get-tuple-element.154) | copy-start | bytes 221188
  104.4 4.6 copy-start.8
  113.3 2.4 copy-start.25
  113.3 5.2 copy-start.27
  113.3 5.2 copy-start.42
  115.7 2.7 copy-start.43
  119.6 2.3 copy-start.18
  120.0 2.2 copy-start.61
  120.0 2.3 copy-start.59
  121.9 163.6 %all-reduce.10.cloned.1.call-start = ((), (), s32[]{:S(2)}) async-start(), calls=%async_computation.11 | async-start | bytes 3538944 | tf_op jit(solution)/shard_map/psum | solution.py:23
  128.9 5.6 copy-start.30
  199.8 3.8 copy-start.13
  203.6 2.4 copy-start
  203.6 2.4 copy-start.54
  203.6 2.5 copy-start.14
  206.1 2.8 copy-start.11
  210.8 105.8 %all-gather.15.cloned.1.call-start = ((), (), s32[]{:S(2)}) async-start(), calls=%async_computation.13 | async-start | bytes 2985984 | tf_op jit(solution)/shard_map/all_gather | solution.py:78
  211.4 137.4 %all-gather.13.cloned.1.call-start = ((), (), s32[]{:S(2)}) async-start(), calls=%async_computation.12 | async-start | bytes 2985984 | tf_op jit(solution)/shard_map/all_gather | solution.py:77
  212.2 223.0 %all-reduce.12.cloned.1.call-start = ((), (), s32[]{:S(2)}) async-start(), calls=%async_computation.14 | async-start | bytes 3538944 | tf_op jit(solution)/shard_map/psum | solution.py:23
  348.8 5.8 copy-start.62
  356.8 3.0 copy-start.55
  356.8 3.0 copy-start.58
  359.5 176.3 %all-reduce.14.cloned.1.call-start = ((), (), s32[]{:S(2)}) async-start(), calls=%async_computation.15 | async-start | bytes 3538944 | tf_op jit(solution)/shard_map/psum | solution.py:23
  435.2 3.3 copy-start.12
  439.1 4.7 copy-start.52
  447.5 4.6 copy-start.20
  447.5 4.6 slice-start
  447.5 4.6 slice-start.1
  461.1 135.5 %all-reduce.16.cloned.1.call-start = ((), (), s32[]{:S(2)}) async-start(), calls=%async_computation.16 | async-start | bytes 2949120 | tf_op jit(solution)/shard_map/psum | solution.py:278
  461.2 2.7 copy-start.21
  469.2 3.1 copy-start.19
  469.2 165.4 %reduce-scatter.16.cloned.1.call-start = ((), (), s32[]{:S(2)}) async-start(), calls=%async_computation.21 | async-start | bytes 995328 | tf_op jit(solution)/shard_map/reduce_scatter | solution.py:315
  472.2 63.6 %copy-start.53 = (f32[16,17]{1,0:T(8,128)S(1)}, f32[16,17]{1,0:T(8,128)}, u32[]{:S(2)}) copy-start(f32[16,17]{1,0:T(8,128)} %copy-done.52) | copy-start | bytes 3268
  472.2 200.7 %reduce-scatter.14.cloned.1.call-start = ((), (), s32[]{:S(2)}) async-start(), calls=%async_computation.20 | async-start | bytes 995328 | tf_op jit(solution)/shard_map/reduce_scatter | solution.py:312
  475.9 65.0 %copy-start.32 = (f32[16,1152]{1,0:T(8,128)S(1)}, f32[16,1152]{1,0:T(8,128)}, u32[]{:S(2)}) copy-start(f32[16,1152]{1,0:T(8,128)} %copy-done.31) | copy-start | bytes 221188
  476.0 236.2 %reduce-scatter.12.cloned.1.call-start = ((), (), s32[]{:S(2)}) async-start(), calls=%async_computation.19 | async-start | bytes 995328 | tf_op jit(solution)/shard_map/reduce_scatter | solution.py:309
  540.9 3.3 copy-start.34
  547.0 212.3 %reduce-scatter.18.cloned.1.call-start = ((), (), s32[]{:S(2)}) async-start(), calls=%async_computation.22 | async-start | bytes 2985984 | tf_op jit(solution)/shard_map/reduce_scatter | solution.py:318
  551.9 254.9 %reduce-scatter.20.cloned.1.call-start = ((), (), s32[]{:S(2)}) async-start(), calls=%async_computation.23 | async-start | bytes 2985984 | tf_op jit(solution)/shard_map/reduce_scatter | solution.py:321
  556.7 387.1 %all-reduce.18.cloned.1.call-start = ((), (), s32[]{:S(2)}) async-start(), calls=%async_computation.24 | async-start | bytes 7077888 | tf_op jit(solution)/shard_map/psum | solution.py:23
  564.0 2.8 copy-start.44
  568.8 1.8 copy-start.16
  581.9 417.3 %reduce-scatter.10.cloned.1.call-start = ((), (), s32[]{:S(2)}) async-start(), calls=%async_computation.18 | async-start | bytes 2985984 | tf_op jit(solution)/shard_map/reduce_scatter | solution.py:306
  591.9 466.9 %reduce-scatter.8.cloned.1.call-start = ((), (), s32[]{:S(2)}) async-start(), calls=%async_computation.17 | async-start | bytes 4423680 | tf_op jit(solution)/shard_map/reduce_scatter | solution.py:302
  611.1 332.8 %copy-start.23 = (f32[16,1152]{1,0:T(8,128)S(1)}, f32[16,1152]{1,0:T(8,128)}, u32[]{:S(2)}) copy-start(f32[16,1152]{1,0:T(8,128)} %copy-done.22) | copy-start | bytes 221188
  761.2 184.8 %copy-start.51 = (f32[16,17]{1,0:T(8,128)S(1)}, f32[16,17]{1,0:T(8,128)}, u32[]{:S(2)}) copy-start(f32[16,17]{1,0:T(8,128)} %copy-done.50) | copy-start | bytes 3268
  943.9 2.1 copy-start.5
  947.5 1.6 copy-start.24
  947.5 1.6 copy-start.37
  949.9 26.2 %copy-start.49 = (f32[4,1152]{1,0:T(4,128)S(1)}, f32[4,1152]{1,0:T(4,128)}, u32[]{:S(2)}) copy-start(f32[4,1152]{1,0:T(4,128)} %param.18) | copy-start | bytes 55300
  (20 other events, 21.3 us)
Sparse Core Ops, SparseCore 0:
  10.0 37.6 all-gather.8
  49.5 36.4 all-gather.6
  87.9 26.5 all-gather.10
  122.0 75.7 all-reduce.7
  211.0 74.5 all-reduce.9
  287.3 29.2 all-gather.14
  318.5 30.2 all-gather.12
  359.6 75.5 all-reduce.11
  461.2 74.5 all-reduce.13
  538.9 57.6 all-reduce.15
  600.2 34.3 reduce-scatter.15
  637.7 35.1 reduce-scatter.13
  677.0 35.0 reduce-scatter.11
  715.5 43.7 reduce-scatter.17
  763.0 43.7 reduce-scatter.19
  809.7 134.1 all-reduce.17
  947.2 42.9 reduce-scatter.9
  992.4 66.3 reduce-scatter.7
where the time goes:
time: 1080 us; the launch traced here: 1070 us
  waiting for transfers between devices  733 us (68%)
  matrix products  105 us (10%)
  blocking collectives  95.8 us (9%)
  local copies, waits for them, and re-layouts  71.9 us (7%)
  other arithmetic  45.7 us (4%)
  between operations  15.4 us (1%)
    psum x5, waiting for transfers between devices, total_rows(): return lax.psum(partial_value, 'tp')  407 us
    reduce_scatter x1, waiting for transfers between devices, shards(): lax.psum_scatter(caption_part.astype(jnp.bfloat16), 'tp', scatter_dimensi...  57.7 us
    reduce_scatter x1, waiting for transfers between devices, shards(): lax.psum_scatter(grad_down.astype(jnp.bfloat16), 'seq', scatter_dimension...  45.7 us
    reduce_scatter x1, waiting for transfers between devices, shards(): lax.psum_scatter(grad_up.astype(jnp.bfloat16), 'seq', scatter_dimension=0...  45.6 us
    reduce_scatter x1, waiting for transfers between devices, shards(): lax.psum_scatter(grad_out.astype(jnp.bfloat16), 'seq', scatter_dimension=...  37.7 us
    reduce_scatter x1, waiting for transfers between devices, shards(): lax.psum_scatter(grad_query2.astype(jnp.bfloat16), 'seq', scatter_dimensi...  36.7 us
    all_gather x1, waiting for transfers between devices, shards(): lax.all_gather(w_up, 'seq', axis=0, tiled=True)  28.1 us
    psum x1, blocking collectives, shards(): lax.psum(d_mods.astype(jnp.bfloat16), 'seq').astype(jnp.float32)  24.9 us
  transfers between devices with their start and end apart: 18, of which 15 were waited for; matrix products, arithmetic and copies ran while one was open for 15% of the time, Pallas kernels for 0%

commit v1 on v0

--- a/solution.py
+++ b/solution.py
@@ -8,6 +8,27 @@
 EPSILON = 1e-06
 NEG_FILL = -1e30
 HIGHEST = lax.Precision.HIGHEST
+
+
+def in_order(blocks, dim):
+    blocks = jnp.moveaxis(blocks, 0, dim)
+    dims = blocks.shape
+    return blocks.reshape(*dims[:dim], dims[dim] * dims[dim + 1], *dims[dim + 2 :])
+
+
+def grow_blocks(x, axis):
+    length, place = (lax.axis_size(axis), lax.axis_index(axis))
+    blocks, stride = (x[None], 1)
+    while stride < length:
+        other = lax.ppermute(blocks, axis, [(i, i ^ stride) for i in range(length)])
+        low = place & stride == 0
+        blocks = jnp.concatenate([jnp.where(low, blocks, other), jnp.where(low, other, blocks)])
+        stride *= 2
+    return blocks
+
+
+def collect(x, axis, dim):
+    return in_order(grow_blocks(x, axis), dim)
 
 
 def normalize(rows):
@@ -76,7 +97,7 @@
         lax.all_gather(w_out2, "seq", axis=1, tiled=True),
         lax.all_gather(w_up, "seq", axis=0, tiled=True),
         lax.all_gather(w_down, "seq", axis=1, tiled=True),
-        lax.all_gather(w_ada, "seq", axis=0, tiled=True),
+        collect(w_ada, "seq", 0),
     )
     qkv_matrix = full_qkv.reshape(width, 3 * inner)
     kv_matrix = full_kv2.reshape(width, 2 * inner)

time: 1080 us -> 1120 us (1.037)
  blocking collectives: 95.8 us -> 161 us
  waiting for transfers between devices: 733 us -> 712 us
    all_gather x1, blocking collectives: 13.7 us -> 59.9 us  [shards(): lax.all_gather(w_query2, 'seq', axis=0, tiled=True)]
    all_gather x1 -> x0, waiting for transfers between devices: 21.8 us -> none  [shards(): lax.all_gather(w_ada, 'seq', axis=0, tiled=True)]
    all_gather x1, blocking collectives: 15 us -> 33.1 us  [shards(): lax.all_gather(w_out, 'seq', axis=1, tiled=True)]
  transfers between devices with their start and end apart: 18 -> 20, of which waited for: 15 -> 15; matrix products, arithmetic and copies ran while one was open for 15% -> 14% of each run, Pallas kernels for 0% -> 0%
where the time goes in v1:
time: 1120 us; the launch traced here: 1110 us
  waiting for transfers between devices  712 us (64%)
  blocking collectives  161 us (14%)
  matrix products  101 us (9%)
  local copies, waits for them, and re-layouts  69.2 us (6%)
  other arithmetic  47.2 us (4%)
  between operations  15.2 us (1%)
    psum x5, waiting for transfers between devices, total_rows(): return lax.psum(partial_value, 'tp')  407 us
    all_gather x1, blocking collectives, shards(): lax.all_gather(w_query2, 'seq', axis=0, tiled=True)  59.9 us
    reduce_scatter x1, waiting for transfers between devices, shards(): lax.psum_scatter(caption_part.astype(jnp.bfloat16), 'tp', scatter_dimensi...  57.7 us
    reduce_scatter x1, waiting for transfers between devices, shards(): lax.psum_scatter(grad_up.astype(jnp.bfloat16), 'seq', scatter_dimension=0...  45.7 us
    reduce_scatter x1, waiting for transfers between devices, shards(): lax.psum_scatter(grad_down.astype(jnp.bfloat16), 'seq', scatter_dimension...  45.7 us
    reduce_scatter x1, waiting for transfers between devices, shards(): lax.psum_scatter(grad_out.astype(jnp.bfloat16), 'seq', scatter_dimension=...  37.5 us
    reduce_scatter x1, waiting for transfers between devices, shards(): lax.psum_scatter(grad_query2.astype(jnp.bfloat16), 'seq', scatter_dimensi...  36.8 us
    all_gather x1, blocking collectives, shards(): lax.all_gather(w_out, 'seq', axis=1, tiled=True)  33.1 us
  transfers between devices with their start and end apart: 20, of which 15 were waited for; matrix products, arithmetic and copies ran while one was open for 14% of the time, Pallas kernels for 0%

profile of v1, /device:TPU:0, one launch (start us, length us, event | category | flops | bytes accessed | tf_op | source)
XLA Modules:
  0.0 1111.0 jit_solution(1296536419223416622)
XLA Ops:
  11.5 2.9 collective-permute-start.1
  14.7 3.7 copy.151
  18.3 3.3 reshape.352
  21.8 33.1 %all_gather.26 = bf16[288,1152]{0,1:T(8,128)(2,1)S(1)} all-gather(bf16[288,144]{0,1:T(8,128)(2,1)S(1)} %copy-done.45), channel_id=1, replica_groups=mesh['seq'=8,'tp'=4] {'seq'}, dimensions={1}, use_global_device_ids=true | all-gather | bytes 746496 | tf_op jit(solution)/shard_map/all_gather | solution.py:94
  58.2 59.9 %all_gather.28 = bf16[1152,288]{1,0:T(8,128)(2,1)} all-gather(bf16[144,288]{1,0:T(8,128)(2,1)S(1)} %copy-done.46), channel_id=1, replica_groups=mesh['seq'=8,'tp'=4] {'seq'}, dimensions={0}, use_global_device_ids=true | all-gather | bytes 746496 | tf_op jit(solution)/shard_map/all_gather | solution.py:95
  118.1 11.4 %all_gather.29 = bf16[288,1152]{0,1:T(8,128)(2,1)} all-gather(bf16[288,144]{0,1:T(8,128)(2,1)S(1)} %copy-done.47), channel_id=1, replica_groups=mesh['seq'=8,'tp'=4] {'seq'}, dimensions={1}, use_global_device_ids=true | all-gather | bytes 746496 | tf_op jit(solution)/shard_map/all_gather | solution.py:97
  133.2 13.7 %all-gather = f32[4,1728,4]{1,2,0:T(4,128)S(1)} all-gather(f32[1,1728,4]{1,2,0:T(4,128)S(1)} %convolution_bitcast_fusion), channel_id=1, replica_groups=mesh['seq'=8,'tp'=4] {'tp'}, dimensions={0}, use_global_device_ids=true | all-gather | bytes 138240 | tf_op jit(solution)/shard_map/all_gather | solution.py:106
  148.7 4.3 copy.144
  153.0 3.3 convolution_convert_fusion.9
  156.3 2.3 reshape.351
  166.4 5.6 copy.152
  172.0 5.6 convolution_convert_fusion.4
  177.6 63.3 %all-reduce.8.cloned.1.call-done = f32[16,17,1152]{2,1,0:T(8,128)} async-done(((f32[16,17,1152]{2,1,0:T(8,128)}), f32[16,17,1152]{2,1,0:T(8,128)}) %all-reduce.8.cloned.1.call-update) | async-done | bytes 1253392 | tf_op jit(solution)/shard_map/psum | solution.py:44
  244.2 2.5 fusion.98
  255.1 73.5 %all-reduce.10.cloned.1.call-done = f32[16,17,1152]{2,1,0:T(8,128)} async-done(((f32[16,17,1152]{2,1,0:T(8,128)}), f32[16,17,1152]{2,1,0:T(8,128)}) %all-reduce.10.cloned.1.call-update) | async-done | bytes 1253392 | tf_op jit(solution)/shard_map/psum | solution.py:44
  328.6 2.5 fusion.94
  334.1 2.2 reshape.358
  336.3 2.3 reshape.356
  338.5 21.2 %all-gather.12.cloned.1.call-done = bf16[1152,1152]{0,1:T(8,128)(2,1)} async-done(((bf16[1152,144]{0,1:T(8,128)(2,1)}), bf16[1152,1152]{0,1:T(8,128)(2,1)}) %all-gather.12.cloned.1.call-update) | async-done | bytes 2654224 | tf_op jit(solution)/shard_map/all_gather | solution.py:99
  359.7 4.1 fusion.99
  363.8 28.0 %all-gather.10.cloned.1.call-done = bf16[1152,1152]{1,0:T(8,128)(2,1)} async-done(((bf16[144,1152]{1,0:T(8,128)(2,1)}), bf16[1152,1152]{1,0:T(8,128)(2,1)}) %all-gather.10.cloned.1.call-update) | async-done | bytes 2654224 | tf_op jit(solution)/shard_map/all_gather | solution.py:98
  391.7 5.0 fusion.36
  397.6 2.2 fusion.100
  399.7 2.7 reshape.359
  402.8 75.4 %all-reduce.12.cloned.1.call-done = f32[16,17,1152]{2,1,0:T(8,128)} async-done(((f32[16,17,1152]{2,1,0:T(8,128)}), f32[16,17,1152]{2,1,0:T(8,128)}) %all-reduce.12.cloned.1.call-update) | async-done | bytes 1253392 | tf_op jit(solution)/shard_map/psum | solution.py:44
  478.1 3.3 multiply_reduce_fusion.2
  484.5 2.2 reshape.360
  486.7 2.6 convolution_convert_fusion.12
  490.4 4.6 multiply_reduce_fusion
  498.9 2.0 dot_general.154
  500.9 3.1 fusion.44
  504.1 2.7 fusion.15
  506.8 4.0 fusion.16
  512.2 2.9 convolution_convert_fusion.5
  516.1 2.8 convolution_convert_fusion.6
  518.9 59.8 %all-reduce.14.cloned.1.call-done = f32[16,17,1152]{2,1,0:T(8,128)} async-done(((f32[16,17,1152]{2,1,0:T(8,128)}), f32[16,17,1152]{2,1,0:T(8,128)}) %all-reduce.14.cloned.1.call-update) | async-done | bytes 1253392 | tf_op jit(solution)/shard_map/psum | solution.py:44
  578.7 3.9 multiply_reduce_fusion.3
  584.9 2.2 reshape.361
  587.2 2.7 convolution_convert_fusion.7
  590.4 4.5 convolution_convert_fusion.1
  594.9 4.8 convolution_convert_fusion
  599.8 4.5 fusion.91
  604.2 2.7 reshape.357
  617.7 2.9 reshape.382
  620.6 4.3 fusion.101
  625.1 2.2 reshape.379
  630.3 4.4 convolution_convert_fusion.3
  634.8 4.9 all-reduce.16.cloned.1.call-done
  639.7 2.6 fusion.52
  643.3 4.2 dot_general.164
  647.5 6.6 convolution_convert_fusion.2
  654.2 23.4 %reduce-scatter.16.cloned.1.call-done = bf16[288,144]{0,1:T(8,128)(2,1)} async-done(((bf16[288,1152]{0,1:T(8,128)(2,1)}), bf16[288,144]{0,1:T(8,128)(2,1)}) %reduce-scatter.16.cloned.1.call-update) | async-done | bytes 82960 | tf_op jit(solution)/shard_map/reduce_scatter | solution.py:336
  679.1 36.8 %reduce-scatter.14.cloned.1.call-done = bf16[144,288]{1,0:T(8,128)(2,1)} async-done(((bf16[1152,288]{1,0:T(8,128)(2,1)}), bf16[144,288]{1,0:T(8,128)(2,1)}) %reduce-scatter.14.cloned.1.call-update) | async-done | bytes 82960 | tf_op jit(solution)/shard_map/reduce_scatter | solution.py:333
  717.5 37.5 %reduce-scatter.12.cloned.1.call-done = bf16[288,144]{0,1:T(8,128)(2,1)} async-done(((bf16[288,1152]{0,1:T(8,128)(2,1)}), bf16[288,144]{0,1:T(8,128)(2,1)}) %reduce-scatter.12.cloned.1.call-update) | async-done | bytes 82960 | tf_op jit(solution)/shard_map/reduce_scatter | solution.py:330
  756.6 45.7 %reduce-scatter.18.cloned.1.call-done = bf16[144,1152]{1,0:T(8,128)(2,1)} async-done(((bf16[1152,1152]{1,0:T(8,128)(2,1)}), bf16[144,1152]{1,0:T(8,128)(2,1)}) %reduce-scatter.18.cloned.1.call-update) | async-done | bytes 331792 | tf_op jit(solution)/shard_map/reduce_scatter | solution.py:339
  804.1 45.7 %reduce-scatter.20.cloned.1.call-done = bf16[1152,144]{0,1:T(8,128)(2,1)} async-done(((bf16[1152,1152]{0,1:T(8,128)(2,1)}), bf16[1152,144]{0,1:T(8,128)(2,1)}) %reduce-scatter.20.cloned.1.call-update) | async-done | bytes 331792 | tf_op jit(solution)/shard_map/reduce_scatter | solution.py:342
  851.6 135.2 %all-reduce.18.cloned.1.call-done = (f32[16,17,1152]{2,1,0:T(8,128)}, f32[16,17,1152]{2,1,0:T(8,128)}) async-done(((f32[16,17,1152]{2,1,0:T(8,128)}, f32[16,17,1152]{2,1,0:T(8,128)}), (f32[16,17,1152]{2,1,0:T(8,128)}, f32[16,17,1152]{2,1,0:T(8,128)})) %all-reduce.18.cloned.1.call-update) | async-done | bytes 2506768 | tf_op jit(solution)/shard_map/psum | solution.py:44
  986.9 2.1 fusion.25
  994.2 24.9 %psum.70 = bf16[4,6912]{1,0:T(4,128)(2,1)S(1)} all-reduce(bf16[4,6912]{1,0:T(4,128)(2,1)S(1)} %bitcast.203), channel_id=1, replica_groups=mesh['seq'=8,'tp'=4] {'seq'}, use_global_device_ids=true, to_apply=%region_31.32 | all-reduce | flops 27648 | bytes 110592 | tf_op jit(solution)/shard_map/psum | solution.py:300
  1019.1 3.4 fusion.68
  1022.5 17.6 %psum.71 = f32[4,1152]{1,0:T(4,128)} all-reduce(f32[4,1152]{1,0:T(4,128)S(1)} %fusion.68), channel_id=1, replica_groups=mesh['seq'=8,'tp'=4] {'tp'}, use_global_device_ids=true, to_apply=%region_32.33 | all-reduce | flops 4608 | bytes 36864 | tf_op jit(solution)/shard_map/psum | solution.py:312
  1040.1 2.1 fusion.73
  1044.1 57.7 %reduce-scatter.8.cloned.1.call-done = bf16[4,300,288]{1,2,0:T(8,128)(2,1)} async-done(((bf16[4,300,1152]{1,2,0:T(8,128)(2,1)}), bf16[4,300,288]{1,2,0:T(8,128)(2,1)}) %reduce-scatter.8.cloned.1.call-update) | async-done | bytes 691216 | tf_op jit(solution)/shard_map/reduce_scatter | solution.py:323
  1101.8 2.5 convert_element_type.205
  (272 shorter events, 80.3 us)
Async XLA Ops:
  7.2 141.5 %all-gather.6.cloned.1.call-start = ((), (), s32[]{:S(2)}) async-start(), calls=%async_computation.7 | async-start | bytes 2985984 | tf_op jit(solution)/shard_map/all_gather | solution.py:93
  7.9 158.5 %all-gather.8.cloned.1.call-start = ((), (), s32[]{:S(2)}) async-start(), calls=%async_computation.9 | async-start | bytes 1990656 | tf_op jit(solution)/shard_map/all_gather | solution.py:96
  8.0 2.3 collective-permute-start
  8.5 6.0 copy-start.59
  11.5 43.4 %collective-permute-start.1 = (bf16[2,144,1728]{2,1,0:T(8,128)(2,1)S(1)}, bf16[2,144,1728]{2,1,0:T(8,128)(2,1)}, u32[]{:S(2)}, u32[]{:S(2)}) collective-permute-start(bf16[2,144,1728]{2,1,0:T(8,128)(2,1)S(1)} %pad_maximum_fusion.3), channel_id=1, source_target_pairs={{0,8},{4,12},{8,0},{12,4},{16,24},{20,28},{24,16},{28,20},{1,9},{5... | collective-permute-start | bytes 2985992 | tf_op jit(solution)/shard_map/ppermute | solution.py:23
  14.4 226.4 %all-reduce.8.cloned.1.call-start = ((), (), s32[]{:S(2)}) async-start(), calls=%async_computation.8 | async-start | bytes 3538944 | tf_op jit(solution)/shard_map/psum | solution.py:44
  18.3 3.3 copy-start.63
  18.3 3.4 copy-start.45
  54.9 108.2 %copy-start.9 = (bf16[288,1152]{0,1:T(8,128)(2,1)}, bf16[288,1152]{0,1:T(8,128)(2,1)S(1)}, u32[]{:S(2)}) copy-start(bf16[288,1152]{0,1:T(8,128)(2,1)S(1)} %all_gather.26) | copy-start | bytes 1990660
  56.6 1.6 copy-start.46
  56.6 61.6 %copy-start.47 = (bf16[288,144]{0,1:T(8,128)(2,1)S(1)}, bf16[288,144]{0,1:T(8,128)(2,1)}, u32[]{:S(2)}) copy-start(bf16[288,144]{0,1:T(8,128)(2,1)} %param.26) | copy-start | bytes 248836
  56.8 72.8 %copy-start.2 = (bf16[16,17,1152]{2,0,1:T(8,128)(2,1)S(1)}, bf16[16,17,1152]{2,0,1:T(8,128)(2,1)}, u32[]{:S(2)}) copy-start(bf16[16,17,1152]{2,0,1:T(8,128)(2,1)} %param.15) | copy-start | bytes 1880068
  56.8 73.5 %copy-start.48 = (f32[4,1152]{1,0:T(4,128)S(1)}, f32[4,1152]{1,0:T(4,128)}, u32[]{:S(2)}) copy-start(f32[4,1152]{1,0:T(4,128)} %param.18) | copy-start | bytes 55300
  56.8 73.5 %collective-permute-start.2 = (bf16[4,144,1728]{2,1,0:T(8,128)(2,1)S(1)}, bf16[4,144,1728]{2,1,0:T(8,128)(2,1)S(1)}, u32[]{:S(2)}, u32[]{:S(2)}) collective-permute-start(bf16[4,144,1728]{2,1,0:T(8,128)(2,1)S(1)} %pad_maximum_fusion.1), channel_id=1, source_target_pairs={{0,16},{4,20},{8,24},{12,28},{16,0},{20,4},{24,8},{28,12},{1,17},{... | collective-permute-start | bytes 5971976 | tf_op jit(solution)/shard_map/ppermute | solution.py:23
  131.2 2.0 copy-start.1
  148.0 5.0 copy-start.22
  148.0 180.7 %copy-start.31 = (f32[16,1152]{1,0:T(8,128)}, f32[16,1152]{1,0:T(8,128)S(1)}, u32[]{:S(2)}) copy-start(f32[16,1152]{1,0:T(8,128)S(1)} %get-tuple-element.165) | copy-start | bytes 221188
  148.0 183.5 %copy-start.36 = (f32[16,1152]{1,0:T(8,128)}, f32[16,1152]{1,0:T(8,128)S(1)}, u32[]{:S(2)}) copy-start(f32[16,1152]{1,0:T(8,128)S(1)} %get-tuple-element.160) | copy-start | bytes 221188
  148.5 4.6 copy-start.10
  158.8 2.8 copy-start.25
  158.8 2.8 copy-start.27
  158.9 2.8 copy-start.42
  162.7 2.3 copy-start.18
  163.1 2.1 copy-start.61
  165.0 163.6 %all-reduce.10.cloned.1.call-start = ((), (), s32[]{:S(2)}) async-start(), calls=%async_computation.10 | async-start | bytes 3538944 | tf_op jit(solution)/shard_map/psum | solution.py:44
  172.0 5.6 copy-start.30
  240.9 2.1 copy-start.11
  242.9 3.8 copy-start.14
  246.7 2.4 copy-start
  246.7 2.4 copy-start.54
  246.7 2.5 copy-start.15
  249.2 2.8 copy-start.12
  253.9 105.8 %all-gather.12.cloned.1.call-start = ((), (), s32[]{:S(2)}) async-start(), calls=%async_computation.12 | async-start | bytes 2985984 | tf_op jit(solution)/shard_map/all_gather | solution.py:99
  254.5 137.2 %all-gather.10.cloned.1.call-start = ((), (), s32[]{:S(2)}) async-start(), calls=%async_computation.11 | async-start | bytes 2985984 | tf_op jit(solution)/shard_map/all_gather | solution.py:98
  255.1 223.0 %all-reduce.12.cloned.1.call-start = ((), (), s32[]{:S(2)}) async-start(), calls=%async_computation.13 | async-start | bytes 3538944 | tf_op jit(solution)/shard_map/psum | solution.py:44
  391.7 5.8 copy-start.62
  399.7 3.0 copy-start.55
  399.7 3.0 copy-start.58
  402.5 176.3 %all-reduce.14.cloned.1.call-start = ((), (), s32[]{:S(2)}) async-start(), calls=%async_computation.14 | async-start | bytes 3538944 | tf_op jit(solution)/shard_map/psum | solution.py:44
  478.1 3.3 copy-start.13
  482.1 4.7 copy-start.52
  490.4 4.6 copy-start.20
  490.4 4.6 slice-start
  490.4 4.6 slice-start.1
  504.0 135.6 %all-reduce.16.cloned.1.call-start = ((), (), s32[]{:S(2)}) async-start(), calls=%async_computation.15 | async-start | bytes 2949120 | tf_op jit(solution)/shard_map/psum | solution.py:299
  504.1 2.7 copy-start.21
  512.1 3.1 copy-start.19
  512.1 165.4 %reduce-scatter.16.cloned.1.call-start = ((), (), s32[]{:S(2)}) async-start(), calls=%async_computation.20 | async-start | bytes 995328 | tf_op jit(solution)/shard_map/reduce_scatter | solution.py:336
  515.1 63.6 %copy-start.53 = (f32[16,17]{1,0:T(8,128)S(1)}, f32[16,17]{1,0:T(8,128)}, u32[]{:S(2)}) copy-start(f32[16,17]{1,0:T(8,128)} %copy-done.52) | copy-start | bytes 3268
  515.1 200.8 %reduce-scatter.14.cloned.1.call-start = ((), (), s32[]{:S(2)}) async-start(), calls=%async_computation.19 | async-start | bytes 995328 | tf_op jit(solution)/shard_map/reduce_scatter | solution.py:333
  518.9 65.0 %copy-start.32 = (f32[16,1152]{1,0:T(8,128)S(1)}, f32[16,1152]{1,0:T(8,128)}, u32[]{:S(2)}) copy-start(f32[16,1152]{1,0:T(8,128)} %copy-done.31) | copy-start | bytes 221188
  518.9 236.1 %reduce-scatter.12.cloned.1.call-start = ((), (), s32[]{:S(2)}) async-start(), calls=%async_computation.18 | async-start | bytes 995328 | tf_op jit(solution)/shard_map/reduce_scatter | solution.py:330
  583.9 3.3 copy-start.34
  589.9 212.3 %reduce-scatter.18.cloned.1.call-start = ((), (), s32[]{:S(2)}) async-start(), calls=%async_computation.21 | async-start | bytes 2985984 | tf_op jit(solution)/shard_map/reduce_scatter | solution.py:339
  594.9 254.9 %reduce-scatter.20.cloned.1.call-start = ((), (), s32[]{:S(2)}) async-start(), calls=%async_computation.22 | async-start | bytes 2985984 | tf_op jit(solution)/shard_map/reduce_scatter | solution.py:342
  599.7 387.1 %all-reduce.18.cloned.1.call-start = ((), (), s32[]{:S(2)}) async-start(), calls=%async_computation.23 | async-start | bytes 7077888 | tf_op jit(solution)/shard_map/psum | solution.py:44
  606.9 2.8 copy-start.44
  611.8 1.8 copy-start.17
  624.8 417.4 %reduce-scatter.10.cloned.1.call-start = ((), (), s32[]{:S(2)}) async-start(), calls=%async_computation.17 | async-start | bytes 2985984 | tf_op jit(solution)/shard_map/reduce_scatter | solution.py:327
  634.8 467.0 %reduce-scatter.8.cloned.1.call-start = ((), (), s32[]{:S(2)}) async-start(), calls=%async_computation.16 | async-start | bytes 4423680 | tf_op jit(solution)/shard_map/reduce_scatter | solution.py:323
  654.1 332.7 %copy-start.23 = (f32[16,1152]{1,0:T(8,128)S(1)}, f32[16,1152]{1,0:T(8,128)}, u32[]{:S(2)}) copy-start(f32[16,1152]{1,0:T(8,128)} %copy-done.22) | copy-start | bytes 221188
  804.1 184.9 %copy-start.51 = (f32[16,17]{1,0:T(8,128)S(1)}, f32[16,17]{1,0:T(8,128)}, u32[]{:S(2)}) copy-start(f32[16,17]{1,0:T(8,128)} %copy-done.50) | copy-start | bytes 3268
  986.9 2.1 copy-start.6
  992.9 26.2 %copy-start.49 = (f32[4,1152]{1,0:T(4,128)S(1)}, f32[4,1152]{1,0:T(4,128)}, u32[]{:S(2)}) copy-start(f32[4,1152]{1,0:T(4,128)} %param.18) | copy-start | bytes 55300
  (23 other events, 26.2 us)
Sparse Core Ops, SparseCore 0:
  9.9 40.9 all-gather.5
  52.8 36.1 all-gather.7
  165.1 75.6 all-reduce.7
  254.1 74.5 all-reduce.9
  330.4 29.2 all-gather.11
  361.4 30.2 all-gather.9
  402.6 75.4 all-reduce.11
  504.2 74.5 all-reduce.13
  582.0 57.6 all-reduce.15
  643.1 34.3 reduce-scatter.15
  680.8 35.0 reduce-scatter.13
  719.9 35.0 reduce-scatter.11
  758.4 43.7 reduce-scatter.17
  806.0 43.7 reduce-scatter.19
  852.6 134.1 all-reduce.17
  990.2 42.9 reduce-scatter.9
  1035.4 66.3 reduce-scatter.7
